TPU v7x, 1024 devices: a whole 4x4x32 slice. The times are simulated.
1024 devices in a mesh: gz: 64 (over y_hi, z), gy: 16 (over x, y_lo, core).
Axes of the slice: x: 4, y: 4 (y_hi: 2, y_lo: 2; y = y_hi * 2 + y_lo), z: 32, core: 2. Of those that a mesh axis runs over, the one named last changes fastest.
Arguments:
- state: bfloat16 [5, 8, 768, 1536], P(None, None, 'gy', 'gz'), may hold values from -6 to 6
- visc_base: bfloat16 [8, 768, 1536], P(None, 'gy', 'gz'), may hold values from 0.29882812 to 3
- dz_op: bfloat16 [1536, 1536], replicated, may hold values from -0.15625 to 0.15625
- dy_op: bfloat16 [768, 768], replicated, may hold values from -0.21875 to 0.21875
Outputs:
- new_state: bfloat16 [5, 8, 768, 1536], P(None, None, 'gy', 'gz')
All inputs are finite; a program needn't handle non-finite values.
Results may differ from a plain program's by a relative error of at most 0.011.
Values may be sent and summed in bfloat16 or wider, within the bound.
No kernel may reach another device: no remote copies, remote signals or barrier semaphores. Data moves between devices by JAX's collectives and lax.ppermute only.
A program may use at most 32 MiB of HBM per device.

v0:
```python
from functools import partial

import jax
import jax.numpy as jnp
from jax import lax
from jax.sharding import Mesh
from jax.sharding import PartitionSpec as P

GZ = ("gz_0", "gz_1")


def in_blocks(value, dim, size):
    shape = value.shape
    pieces = value.reshape(*shape[:dim], size, shape[dim] // size, *shape[dim + 1 :])
    return jnp.moveaxis(pieces, dim, 0)


def joined_along(pieces, dim):
    shape = list(pieces.shape[1:])
    shape[dim] *= pieces.shape[0]
    return jnp.moveaxis(pieces, 0, dim).reshape(shape)


def turned_blocks(pieces, axes, order):
    shape = [lax.axis_size(a) for a in axes]
    pieces = pieces.reshape(*shape, *pieces.shape[1:])
    for k in order:
        pieces = lax.all_to_all(pieces, axes[k], split_axis=k, concat_axis=k, tiled=True)
    return pieces.reshape(-1, *pieces.shape[len(axes) :])


def exchange_by_axis(value, axes, order, split_dim, concat_dim):
    pieces = in_blocks(value, split_dim, lax.axis_size(axes))
    return joined_along(turned_blocks(pieces, axes, order), concat_dim)


def apply_line(items, operator):
    shape_in = items.shape
    result = jnp.dot(
        items.reshape(-1, operator.shape[0]), operator, preferred_element_type=jnp.float32
    )
    return result.astype(jnp.bfloat16).reshape(shape_in)


def into_zlines(values, handler):
    layers, planes, ylocal, zlocal = values.shape
    flattened = values.reshape(layers, planes * ylocal, zlocal)
    return handler(lax.all_to_all(flattened, GZ, split_axis=1, concat_axis=2, tiled=True))


def from_zlines(values, planes, ylocal):
    returned = exchange_by_axis(values, GZ, (0, 1), 2, 1)
    return returned.reshape(returned.shape[0], planes, ylocal, returned.shape[2])


def into_ylines(values, handler):
    layers, planes, ylocal, zlocal = values.shape
    turned = jnp.swapaxes(values, 2, 3).reshape(layers, planes * zlocal, ylocal)
    return handler(lax.all_to_all(turned, "gy", split_axis=1, concat_axis=2, tiled=True))


def from_ylines(values, planes, zlocal):
    returned = lax.all_to_all(values, "gy", split_axis=2, concat_axis=1, tiled=True)
    layers = returned.shape[0]
    return jnp.swapaxes(returned.reshape(layers, planes, zlocal, returned.shape[2]), 2, 3)


def viscosity(dens_y, dens_z, visc_base):
    sensor = dens_y.astype(jnp.float32) ** 2 + dens_z.astype(jnp.float32) ** 2
    return (visc_base.astype(jnp.float32) * (0.5 + sensor / (1.0 + sensor))).astype(jnp.bfloat16)


def product(visc, gradient):
    return (visc.astype(jnp.float32) * gradient.astype(jnp.float32)).astype(jnp.bfloat16)


def on_device(state, visc_base, dz_op, dy_op):
    planes, ylocal, zlocal = visc_base.shape
    zderive = partial(apply_line, operator=dz_op)
    yderive = partial(apply_line, operator=dy_op)
    grad_z = from_zlines(into_zlines(state, zderive), planes, ylocal)
    grad_y = from_ylines(into_ylines(state, yderive), planes, zlocal)
    visc = viscosity(grad_y[0], grad_z[0], visc_base)
    div_z = from_zlines(into_zlines(product(visc[None], grad_z), zderive), planes, ylocal)
    div_y = from_ylines(into_ylines(product(visc[None], grad_y), yderive), planes, zlocal)
    total = state.astype(jnp.float32) + 0.5 * (
        div_y.astype(jnp.float32) + div_z.astype(jnp.float32)
    )
    return total.astype(jnp.bfloat16)


def solution(mesh):
    finer = Mesh(mesh.devices.reshape(2, 32, mesh.shape["gy"]), ("gz_0", "gz_1", "gy"))
    return jax.shard_map(
        on_device,
        mesh=finer,
        in_specs=(P(None, None, "gy", GZ), P(None, "gy", GZ), P(), P()),
        out_specs=P(None, None, "gy", GZ),
        check_vma=False,
    )
```

profile of v0, /device:TPU:1, one launch (start us, length us, event | category | flops | bytes accessed | tf_op | source)
XLA Modules:
  0.0 245.4 jit_solution(8263263845754850085)
XLA Ops:
  0.0 1.2 copy.95
  1.2 1.0 reshape.94
  2.2 17.4 %all-to-all-start = ((bf16[16,2,1440]{2,1,0:T(2,128)(2,1)}), bf16[16,2,1440]{2,1,0:T(2,128)(2,1)S(1)}, u32[]{:S(2)}, u32[]{:S(2)}) async-start(bf16[16,2,1440]{2,1,0:T(2,128)(2,1)} %reshape.94), calls=%async_computation | async-start | bytes 196608 | tf_op jit(solution)/shard_map/all_to_all | solution.py:59
  19.6 1.4 copy.133
  21.0 1.3 reshape.88
  22.4 3.2 %all-to-all-done = bf16[16,2,1440]{2,1,0:T(2,128)(2,1)S(1)} async-done(((bf16[16,2,1440]{2,1,0:T(2,128)(2,1)}), bf16[16,2,1440]{2,1,0:T(2,128)(2,1)S(1)}, u32[]{:S(2)}, u32[]{:S(2)}) %all-to-all-start) | async-done | bytes 92192 | tf_op jit(solution)/shard_map/all_to_all | solution.py:59
  25.6 20.8 %all-to-all-start.2 = ((bf16[64,2,360]{2,1,0:T(2,128)(2,1)}), bf16[64,2,360]{2,1,0:T(2,128)(2,1)S(1)}, u32[]{:S(2)}, u32[]{:S(2)}) async-start(bf16[64,2,360]{2,1,0:T(2,128)(2,1)} %reshape.88), calls=%async_computation.2 | async-start | bytes 196608 | tf_op jit(solution)/shard_map/all_to_all | solution.py:48
  46.4 0.3 reshape.95
  47.1 26.7 %all-to-all-done.2 = bf16[64,2,360]{2,1,0:T(2,128)(2,1)S(1)} async-done(((bf16[64,2,360]{2,1,0:T(2,128)(2,1)}), bf16[64,2,360]{2,1,0:T(2,128)(2,1)S(1)}, u32[]{:S(2)}, u32[]{:S(2)}) %all-to-all-start.2) | async-done | bytes 92192 | tf_op jit(solution)/shard_map/all_to_all | solution.py:48
  73.8 0.5 reshape.89
  74.4 0.7 reshape.75
  75.1 3.2 %convolution_convert_fusion.1 = bf16[30,1536]{1,0:T(8,128)(2,1)S(1)} fusion(bf16[30,1536]{1,0:T(8,128)(2,1)S(1)} %reshape.75, bf16[1536,1536]{1,0:T(8,128)(2,1)} %param.6), kind=kOutput, calls=%fused_computation.1 | convolution fusion | flops 141603840 | bytes 4902912 | tf_op jit(solution)/shard_map/dot_general | solution.py:39
  78.4 0.8 reshape_reshape.8
  79.4 0.9 reshape.90
  80.3 3.3 %all-to-all-start.3 = ((bf16[2,2,11520]{2,1,0:T(2,128)(2,1)}), bf16[2,2,11520]{2,1,0:T(2,128)(2,1)S(1)}, u32[]{:S(2)}, u32[]{:S(2)}) async-start(bf16[2,2,11520]{2,1,0:T(2,128)(2,1)} %reshape.90), calls=%async_computation.3 | async-start | bytes 184320 | tf_op jit(solution)/shard_map/all_to_all | solution.py:28
  84.0 1.1 copy.98
  85.1 1.8 reshape.96
  87.0 1.3 all-to-all-done.3
  88.3 7.9 %all-to-all-start.1 = ((bf16[16,2,1440]{2,1,0:T(2,128)(2,1)}), bf16[16,2,1440]{2,1,0:T(2,128)(2,1)S(1)}, u32[]{:S(2)}, u32[]{:S(2)}) async-start(bf16[16,2,1440]{2,1,0:T(2,128)(2,1)} %reshape.96), calls=%async_computation.1 | async-start | bytes 196608 | tf_op jit(solution)/shard_map/all_to_all | solution.py:63
  96.3 0.5 copy.106
  96.9 1.2 reshape.92
  98.1 4.0 %all-to-all-done.1 = bf16[16,2,1440]{2,1,0:T(2,128)(2,1)S(1)} async-done(((bf16[16,2,1440]{2,1,0:T(2,128)(2,1)}), bf16[16,2,1440]{2,1,0:T(2,128)(2,1)S(1)}, u32[]{:S(2)}, u32[]{:S(2)}) %all-to-all-start.1) | async-done | bytes 92192 | tf_op jit(solution)/shard_map/all_to_all | solution.py:63
  102.1 4.0 %all-to-all-start.4 = ((bf16[32,2,720]{2,1,0:T(2,128)(2,1)}), bf16[32,2,720]{2,1,0:T(2,128)(2,1)S(1)}, u32[]{:S(2)}, u32[]{:S(2)}) async-start(bf16[32,2,720]{2,1,0:T(2,128)(2,1)} %reshape.92), calls=%async_computation.4 | async-start | bytes 196608 | tf_op jit(solution)/shard_map/all_to_all | solution.py:28
  106.1 1.2 reshape.97
  107.3 1.1 copy.100
  108.5 1.1 copy.131
  109.8 23.0 %all-to-all-done.4 = bf16[32,2,720]{2,1,0:T(2,128)(2,1)S(1)} async-done(((bf16[32,2,720]{2,1,0:T(2,128)(2,1)}), bf16[32,2,720]{2,1,0:T(2,128)(2,1)S(1)}, u32[]{:S(2)}, u32[]{:S(2)}) %all-to-all-start.4) | async-done | bytes 92192 | tf_op jit(solution)/shard_map/all_to_all | solution.py:28
  132.8 0.4 reshape.93
  133.2 0.7 copy.107
  134.5 0.8 copy.138
  135.5 1.0 reshape.104
  136.5 6.6 %all-to-all-start.5 = ((bf16[16,2,1440]{2,1,0:T(2,128)(2,1)}), bf16[16,2,1440]{2,1,0:T(2,128)(2,1)}, u32[]{:S(2)}, u32[]{:S(2)}) async-start(bf16[16,2,1440]{2,1,0:T(2,128)(2,1)} %reshape.104), calls=%async_computation.5 | async-start | bytes 196608 | tf_op jit(solution)/shard_map/all_to_all | solution.py:59
  143.2 0.5 copy.119
  143.8 1.0 multiply_convert_fusion
  144.8 0.4 copy.145
  145.2 1.3 reshape.98
  146.5 2.8 %all-to-all-done.5 = bf16[16,2,1440]{2,1,0:T(2,128)(2,1)} async-done(((bf16[16,2,1440]{2,1,0:T(2,128)(2,1)}), bf16[16,2,1440]{2,1,0:T(2,128)(2,1)}, u32[]{:S(2)}, u32[]{:S(2)}) %all-to-all-start.5) | async-done | bytes 92192 | tf_op jit(solution)/shard_map/all_to_all | solution.py:59
  149.3 4.6 %all-to-all-start.7 = ((bf16[64,2,360]{2,1,0:T(2,128)(2,1)}), bf16[64,2,360]{2,1,0:T(2,128)(2,1)S(1)}, u32[]{:S(2)}, u32[]{:S(2)}) async-start(bf16[64,2,360]{2,1,0:T(2,128)(2,1)} %reshape.98), calls=%async_computation.7 | async-start | bytes 196608 | tf_op jit(solution)/shard_map/all_to_all | solution.py:48
  153.9 1.2 reshape.105
  155.5 26.5 %all-to-all-done.7 = bf16[64,2,360]{2,1,0:T(2,128)(2,1)S(1)} async-done(((bf16[64,2,360]{2,1,0:T(2,128)(2,1)}), bf16[64,2,360]{2,1,0:T(2,128)(2,1)S(1)}, u32[]{:S(2)}, u32[]{:S(2)}) %all-to-all-start.7) | async-done | bytes 92192 | tf_op jit(solution)/shard_map/all_to_all | solution.py:48
  182.0 0.5 reshape.99
  182.6 0.7 reshape.80
  183.3 3.2 %convolution_convert_fusion = bf16[30,1536]{1,0:T(8,128)(2,1)S(1)} fusion(bf16[30,1536]{1,0:T(8,128)(2,1)S(1)} %reshape.80, bf16[1536,1536]{1,0:T(8,128)(2,1)} %param.6), kind=kOutput, calls=%fused_computation | convolution fusion | flops 141603840 | bytes 4902912 | tf_op jit(solution)/shard_map/dot_general | solution.py:39
  186.5 0.8 reshape_reshape.9
  187.5 0.9 reshape.100
  188.5 3.6 %all-to-all-start.8 = ((bf16[2,2,11520]{2,1,0:T(2,128)(2,1)}), bf16[2,2,11520]{2,1,0:T(2,128)(2,1)S(1)}, u32[]{:S(2)}, u32[]{:S(2)}) async-start(bf16[2,2,11520]{2,1,0:T(2,128)(2,1)} %reshape.100), calls=%async_computation.8 | async-start | bytes 184320 | tf_op jit(solution)/shard_map/all_to_all | solution.py:28
  192.4 1.1 copy.114
  193.5 1.8 reshape.106
  195.3 1.1 all-to-all-done.8
  196.4 7.2 %all-to-all-start.6 = ((bf16[16,2,1440]{2,1,0:T(2,128)(2,1)}), bf16[16,2,1440]{2,1,0:T(2,128)(2,1)S(1)}, u32[]{:S(2)}, u32[]{:S(2)}) async-start(bf16[16,2,1440]{2,1,0:T(2,128)(2,1)} %reshape.106), calls=%async_computation.6 | async-start | bytes 196608 | tf_op jit(solution)/shard_map/all_to_all | solution.py:63
  203.8 0.5 copy.124
  204.4 1.2 reshape.102
  205.6 4.0 %all-to-all-done.6 = bf16[16,2,1440]{2,1,0:T(2,128)(2,1)S(1)} async-done(((bf16[16,2,1440]{2,1,0:T(2,128)(2,1)}), bf16[16,2,1440]{2,1,0:T(2,128)(2,1)S(1)}, u32[]{:S(2)}, u32[]{:S(2)}) %all-to-all-start.6) | async-done | bytes 92192 | tf_op jit(solution)/shard_map/all_to_all | solution.py:63
  209.6 3.9 %all-to-all-start.9 = ((bf16[32,2,720]{2,1,0:T(2,128)(2,1)}), bf16[32,2,720]{2,1,0:T(2,128)(2,1)S(1)}, u32[]{:S(2)}, u32[]{:S(2)}) async-start(bf16[32,2,720]{2,1,0:T(2,128)(2,1)} %reshape.102), calls=%async_computation.9 | async-start | bytes 196608 | tf_op jit(solution)/shard_map/all_to_all | solution.py:28
  213.5 1.2 reshape.107
  214.6 0.8 copy.115
  215.9 0.8 reshape.85
  216.7 24.5 %all-to-all-done.9 = bf16[32,2,720]{2,1,0:T(2,128)(2,1)S(1)} async-done(((bf16[32,2,720]{2,1,0:T(2,128)(2,1)}), bf16[32,2,720]{2,1,0:T(2,128)(2,1)S(1)}, u32[]{:S(2)}, u32[]{:S(2)}) %all-to-all-start.9) | async-done | bytes 92192 | tf_op jit(solution)/shard_map/all_to_all | solution.py:28
  241.2 0.4 reshape.103
  241.6 0.5 copy.125
  242.4 0.4 reshape.86
  242.9 0.5 copy.127
  243.8 0.6 copy-done.1
  244.6 0.8 fusion.2
  (40 shorter events, 5.2 us)
Async XLA Ops:
  0.0 83.6 %copy-start = (bf16[768,768]{1,0:T(8,128)(2,1)S(1)}, bf16[768,768]{1,0:T(8,128)(2,1)}, u32[]{:S(2)}) copy-start(bf16[768,768]{1,0:T(8,128)(2,1)} %param.7) | copy-start | bytes 3538948
  2.2 23.4 %all-to-all-start = ((bf16[16,2,1440]{2,1,0:T(2,128)(2,1)}), bf16[16,2,1440]{2,1,0:T(2,128)(2,1)S(1)}, u32[]{:S(2)}, u32[]{:S(2)}) async-start(bf16[16,2,1440]{2,1,0:T(2,128)(2,1)} %reshape.94), calls=%async_computation | async-start | bytes 196608 | tf_op jit(solution)/shard_map/all_to_all | solution.py:59
  25.6 48.2 %all-to-all-start.2 = ((bf16[64,2,360]{2,1,0:T(2,128)(2,1)}), bf16[64,2,360]{2,1,0:T(2,128)(2,1)S(1)}, u32[]{:S(2)}, u32[]{:S(2)}) async-start(bf16[64,2,360]{2,1,0:T(2,128)(2,1)} %reshape.88), calls=%async_computation.2 | async-start | bytes 196608 | tf_op jit(solution)/shard_map/all_to_all | solution.py:48
  80.3 7.9 %all-to-all-start.3 = ((bf16[2,2,11520]{2,1,0:T(2,128)(2,1)}), bf16[2,2,11520]{2,1,0:T(2,128)(2,1)S(1)}, u32[]{:S(2)}, u32[]{:S(2)}) async-start(bf16[2,2,11520]{2,1,0:T(2,128)(2,1)} %reshape.90), calls=%async_computation.3 | async-start | bytes 184320 | tf_op jit(solution)/shard_map/all_to_all | solution.py:28
  88.3 13.8 %all-to-all-start.1 = ((bf16[16,2,1440]{2,1,0:T(2,128)(2,1)}), bf16[16,2,1440]{2,1,0:T(2,128)(2,1)S(1)}, u32[]{:S(2)}, u32[]{:S(2)}) async-start(bf16[16,2,1440]{2,1,0:T(2,128)(2,1)} %reshape.96), calls=%async_computation.1 | async-start | bytes 196608 | tf_op jit(solution)/shard_map/all_to_all | solution.py:63
  102.1 30.8 %all-to-all-start.4 = ((bf16[32,2,720]{2,1,0:T(2,128)(2,1)}), bf16[32,2,720]{2,1,0:T(2,128)(2,1)S(1)}, u32[]{:S(2)}, u32[]{:S(2)}) async-start(bf16[32,2,720]{2,1,0:T(2,128)(2,1)} %reshape.92), calls=%async_computation.4 | async-start | bytes 196608 | tf_op jit(solution)/shard_map/all_to_all | solution.py:28
  133.2 1.2 copy-start.3
  136.5 12.7 %all-to-all-start.5 = ((bf16[16,2,1440]{2,1,0:T(2,128)(2,1)}), bf16[16,2,1440]{2,1,0:T(2,128)(2,1)}, u32[]{:S(2)}, u32[]{:S(2)}) async-start(bf16[16,2,1440]{2,1,0:T(2,128)(2,1)} %reshape.104), calls=%async_computation.5 | async-start | bytes 196608 | tf_op jit(solution)/shard_map/all_to_all | solution.py:59
  149.3 32.7 %all-to-all-start.7 = ((bf16[64,2,360]{2,1,0:T(2,128)(2,1)}), bf16[64,2,360]{2,1,0:T(2,128)(2,1)S(1)}, u32[]{:S(2)}, u32[]{:S(2)}) async-start(bf16[64,2,360]{2,1,0:T(2,128)(2,1)} %reshape.98), calls=%async_computation.7 | async-start | bytes 196608 | tf_op jit(solution)/shard_map/all_to_all | solution.py:48
  188.5 7.9 %all-to-all-start.8 = ((bf16[2,2,11520]{2,1,0:T(2,128)(2,1)}), bf16[2,2,11520]{2,1,0:T(2,128)(2,1)S(1)}, u32[]{:S(2)}, u32[]{:S(2)}) async-start(bf16[2,2,11520]{2,1,0:T(2,128)(2,1)} %reshape.100), calls=%async_computation.8 | async-start | bytes 184320 | tf_op jit(solution)/shard_map/all_to_all | solution.py:28
  196.4 13.2 %all-to-all-start.6 = ((bf16[16,2,1440]{2,1,0:T(2,128)(2,1)}), bf16[16,2,1440]{2,1,0:T(2,128)(2,1)S(1)}, u32[]{:S(2)}, u32[]{:S(2)}) async-start(bf16[16,2,1440]{2,1,0:T(2,128)(2,1)} %reshape.106), calls=%async_computation.6 | async-start | bytes 196608 | tf_op jit(solution)/shard_map/all_to_all | solution.py:63
  209.6 31.6 %all-to-all-start.9 = ((bf16[32,2,720]{2,1,0:T(2,128)(2,1)}), bf16[32,2,720]{2,1,0:T(2,128)(2,1)S(1)}, u32[]{:S(2)}, u32[]{:S(2)}) async-start(bf16[32,2,720]{2,1,0:T(2,128)(2,1)} %reshape.102), calls=%async_computation.9 | async-start | bytes 196608 | tf_op jit(solution)/shard_map/all_to_all | solution.py:28
  243.5 0.9 copy-start.1
  243.5 1.2 copy-start.2
where the time goes:
time: 246 us; the launch traced here: 245 us
  waiting for transfers between devices  117 us (48%)
  starting transfers between devices  79.3 us (32%)
  local copies, waits for them, and re-layouts  39.5 us (16%)
  matrix products  7.13 us (3%)
    all_to_all x2, waiting for transfers between devices, into_zlines(): lax.all_to_all(flattened, GZ, split_axis=1, concat_axis=2, tiled=True)  53.2 us
    all_to_all x4, waiting for transfers between devices, turned_blocks(): lax.all_to_all(pieces, axes[k], split_axis=k, concat_axis=k, tiled=True)  49.9 us
    all_to_all x2, starting transfers between devices, into_zlines(): lax.all_to_all(flattened, GZ, split_axis=1, concat_axis=2, tiled=True)  25.4 us
    all_to_all x2, starting transfers between devices, into_ylines(): lax.all_to_all(turned, 'gy', split_axis=1, concat_axis=2, tiled=True)  24.1 us
    unnamed x28, local copies, waits for them, and re-layouts  19.6 us
    all_to_all x2, starting transfers between devices, from_ylines(): lax.all_to_all(values, 'gy', split_axis=2, concat_axis=1, tiled=True)  15.1 us
    all_to_all x4, starting transfers between devices, turned_blocks(): lax.all_to_all(pieces, axes[k], split_axis=k, concat_axis=k, tiled=True)  14.8 us
    all_to_all x2, waiting for transfers between devices, from_ylines(): lax.all_to_all(values, 'gy', split_axis=2, concat_axis=1, tiled=True)  7.99 us
  transfers between devices with their start and end apart: 10, of which 10 were waited for; matrix products, arithmetic and copies ran while one was open for 10% of the time, Pallas kernels for 0%

commit v1 on v0

v1 whole, which is shorter than its diff:
```python
import jax
import jax.numpy as jnp
from jax import lax
from jax.sharding import PartitionSpec as P

F32 = jnp.float32
BF16 = jnp.bfloat16


def spread(block, axis):
    n = lax.axis_size(axis)
    copies = jnp.broadcast_to(block[None], (n, *block.shape))
    return lax.all_to_all(copies, axis, split_axis=0, concat_axis=0, tiled=True)


def rounded(left, right, dims):
    return lax.dot_general(left, right, (dims, ((), ())), preferred_element_type=F32).astype(BF16)


def on_device(state, visc_base, dz_op, dy_op):
    fields, planes, ylocal, zlocal = state.shape
    gz, gy = lax.axis_size("gz"), lax.axis_size("gy")
    ny, nz = dy_op.shape[0], dz_op.shape[0]
    parts = gz // planes
    lines = ylocal // parts
    cols = planes * zlocal

    st = jnp.transpose(state, (2, 0, 1, 3)).reshape(ylocal, fields * cols)
    vb = jnp.transpose(visc_base, (1, 0, 2)).reshape(ylocal, cols)
    whole = spread(st, "gy").reshape(ny, fields * cols)
    own = lax.dynamic_slice_in_dim(dy_op, lax.axis_index("gy") * ylocal, ylocal, 1)
    dens_y = rounded(own, whole[:, :cols], ((0,), (0,)))

    out = jnp.concatenate([st, dens_y, vb], axis=1)
    out = out.reshape(parts, lines, fields + 2, planes, zlocal)
    out = jnp.transpose(out, (3, 0, 2, 1, 4)).reshape(gz, (fields + 2) * lines * zlocal)
    got = lax.all_to_all(out, "gz", split_axis=0, concat_axis=0, tiled=True)
    got = got.reshape(gz, (fields + 2) * lines, zlocal)
    got = jnp.transpose(got, (1, 0, 2)).reshape((fields + 2) * lines, nz)
    grad_z = rounded(got[: fields * lines], dz_op, ((1,), (0,)))
    gz0 = grad_z[:lines].astype(F32)
    gy0 = got[fields * lines : (fields + 1) * lines].astype(F32)
    base = got[(fields + 1) * lines :].astype(F32)
    sensor = gy0**2 + gz0**2
    visc = (base * (0.5 + sensor / (1.0 + sensor))).astype(BF16)
    flux_z = (visc.astype(F32)[None] * grad_z.reshape(fields, lines, nz).astype(F32)).astype(BF16)
    div_z = rounded(flux_z.reshape(fields * lines, nz), dz_op, ((1,), (0,)))

    ret = jnp.concatenate([div_z, visc], axis=0).reshape((fields + 1) * lines, gz, zlocal)
    ret = jnp.transpose(ret, (1, 0, 2)).reshape(gz, (fields + 1) * lines * zlocal)
    ret = lax.all_to_all(ret, "gz", split_axis=0, concat_axis=0, tiled=True)
    ret = ret.reshape(planes, parts, fields + 1, lines, zlocal)
    ret = jnp.transpose(ret, (1, 3, 2, 0, 4)).reshape(ylocal, (fields + 1) * cols)

    grad_y = rounded(dy_op, whole, ((0,), (0,)))
    visc_all = spread(ret[:, fields * cols :], "gy").reshape(ny, cols)
    flux_y = (visc_all.astype(F32)[:, None] * grad_y.reshape(ny, fields, cols).astype(F32)).astype(BF16)
    div_y = rounded(own, flux_y.reshape(ny, fields * cols), ((0,), (0,)))
    total = st.astype(F32) + 0.5 * (div_y.astype(F32) + ret[:, : fields * cols].astype(F32))
    total = total.astype(BF16).reshape(ylocal, fields, planes, zlocal)
    return jnp.transpose(total, (1, 2, 0, 3))


def solution(mesh):
    return jax.shard_map(
        on_device,
        mesh=mesh,
        in_specs=(P(None, None, "gy", "gz"), P(None, "gy", "gz"), P(), P()),
        out_specs=P(None, None, "gy", "gz"),
        check_vma=False,
    )
```

time: 246 us -> 179 us (0.73)
  blocking collectives: 0 us -> 103 us
  waiting for transfers between devices: 117 us -> 21.2 us
  starting transfers between devices: 79.3 us -> 17.7 us
  local copies, waits for them, and re-layouts: 39.5 us -> 21.8 us
  other arithmetic: 1.94 us -> 5.08 us
  matrix products: 7.13 us -> 9.87 us
    all_to_all x0 -> x3, blocking collectives: none -> 103 us  [the longest x1 49.7 us: on_device(): got = lax.all_to_all(out, 'gz', split_axis=0, concat_axis=0, tiled=True)]
    all_to_all x10 -> x1, waiting for transfers between devices: 117 us -> 21.2 us  [spread(): return lax.all_to_all(copies, axis, split_axis=0, concat_axis=0, tiled=True)]
    all_to_all x10 -> x1, starting transfers between devices: 79.3 us -> 17.7 us  [spread(): return lax.all_to_all(copies, axis, split_axis=0, concat_axis=0, tiled=True)]
    unnamed x28 -> x19, local copies, waits for them, and re-layouts: 19.6 us -> 1.41 us
    all_to_all x0 -> x3, other arithmetic: none -> 4.29 us  [the longest x2 2.95 us: on_device(): ret = lax.all_to_all(ret, 'gz', split_axis=0, concat_axis=0, tiled=True)]
    dot_general x4 -> x5, matrix products: 7.13 us -> 9.87 us  [rounded(): lax.dot_general(left, right, (dims, ((), ())), preferred_element_type=F32)]
    all_to_all x11 -> x3, local copies, waits for them, and re-layouts: 5.63 us -> 3.13 us  [on_device(): got = lax.all_to_all(out, 'gz', split_axis=0, concat_axis=0, tiled=True)]
    reshape x13 -> x6, local copies, waits for them, and re-layouts: 6.29 us -> 6.92 us  [the longest x1 1.65 us: on_device(): ret = ret.reshape(planes, parts, fields + 1, lines, zlocal)]
  transfers between devices with their start and end apart: 10 -> 1, of which waited for: 10 -> 1; matrix products, arithmetic and copies ran while one was open for 10% -> 0% of each run, Pallas kernels for 0% -> 0%
where the time goes in v1:
time: 179 us
  blocking collectives  103 us (58%)
  local copies, waits for them, and re-layouts  21.8 us (12%)
  waiting for transfers between devices  21.2 us (12%)
  starting transfers between devices  17.7 us (10%)
  matrix products  9.87 us (6%)
  other arithmetic  5.08 us (3%)
    all_to_all x1, blocking collectives, on_device(): got = lax.all_to_all(out, 'gz', split_axis=0, concat_axis=0, tiled=True)  49.7 us
    all_to_all x1, blocking collectives, on_device(): ret = lax.all_to_all(ret, 'gz', split_axis=0, concat_axis=0, tiled=True)  36.1 us
    all_to_all x1, waiting for transfers between devices, spread(): return lax.all_to_all(copies, axis, split_axis=0, concat_axis=0, tiled=True)  21.2 us
    all_to_all x1, starting transfers between devices, spread(): return lax.all_to_all(copies, axis, split_axis=0, concat_axis=0, tiled=True)  17.7 us
    all_to_all x1, blocking collectives, spread(): return lax.all_to_all(copies, axis, split_axis=0, concat_axis=0, tiled=True)  17 us
    dot_general x5, matrix products, rounded(): lax.dot_general(left, right, (dims, ((), ())), preferred_element_type=F32)  9.87 us
  transfers between devices with their start and end apart: 1, of which 1 were waited for; matrix products, arithmetic and copies ran while one was open for 0% of the time, Pallas kernels for 0%

profile of v1, /device:TPU:1, one launch (start us, length us, event | category | flops | bytes accessed | tf_op | source)
XLA Modules:
  0.0 178.7 jit_solution(12610523529970283690)
XLA Ops:
  0.0 0.0 copy-start
  0.0 1.2 copy.35
  1.2 0.0 copy-start.1
  1.2 1.4 broadcast_in_dim.4
  2.5 0.0 copy-start.6
  2.5 17.7 %all-to-all-start = ((bf16[16,48,960]{2,1,0:T(8,128)(2,1)}), bf16[16,48,960]{2,1,0:T(8,128)(2,1)S(1)}, u32[]{:S(2)}, u32[]{:S(2)}) async-start(bf16[16,48,960]{2,1,0:T(8,128)(2,1)} %broadcast_in_dim.4), calls=%async_computation | async-start | bytes 3145728 | tf_op jit(solution)/shard_map/all_to_all | solution.py:13
  20.3 0.0 copy-done.6
  20.3 0.1 copy.38
  20.4 21.2 %all-to-all-done = bf16[16,48,960]{2,1,0:T(8,128)(2,1)S(1)} async-done(((bf16[16,48,960]{2,1,0:T(8,128)(2,1)}), bf16[16,48,960]{2,1,0:T(8,128)(2,1)S(1)}, u32[]{:S(2)}, u32[]{:S(2)}) %all-to-all-start) | async-done | bytes 1474592 | tf_op jit(solution)/shard_map/all_to_all | solution.py:13
  41.6 0.0 copy-done
  41.6 0.3 convolution_convert_fusion.4
  41.9 0.0 copy-done.1
  41.9 0.7 concatenate.6
  42.6 1.5 reshape.65
  44.1 1.1 copy.39
  45.2 2.4 %all_to_all.24 = bf16[64,1,1008]{2,1,0:T(2,128)(2,1)S(1)} reshape(bf16[8,8,7,6,24]{4,3,2,1,0:T(8,128)(2,1)} %copy.39) | data formatting | bytes 258048 | tf_op jit(solution)/shard_map/all_to_all | solution.py:37
  47.6 0.5 broadcast.5
  48.2 1.3 reduce.1
  49.5 0.2 reshape.74
  49.7 49.7 %all_to_all.29 = bf16[64,2,504]{2,1,0:T(2,128)(2,1)S(1)} all-to-all(bf16[64,2,504]{2,1,0:T(2,128)(2,1)S(1)} %reshape.74), channel_id=1, replica_groups=mesh['gz'=64,'gy'=16] {'gz'}, dimensions={0} | all-to-all | bytes 258048 | tf_op jit(solution)/shard_map/all_to_all | solution.py:37
  99.3 0.2 reshape.75
  99.5 0.2 copy.41
  99.8 0.6 slice_convert_fusion
  100.4 1.0 copy.42
  101.4 0.8 reshape.71
  102.2 0.1 copy.43
  102.3 0.1 integer_pow.10
  102.5 0.3 copy.44
  102.7 0.7 slice.30
  103.4 0.0 copy-start.5
  103.4 3.2 %convolution_convert_fusion.1 = bf16[30,1536]{1,0:T(8,128)(2,1)S(1)} fusion(bf16[30,1536]{1,0:T(8,128)(2,1)S(1)} %slice.30, bf16[1536,1536]{1,0:T(8,128)(2,1)} %param.6), kind=kOutput, calls=%fused_computation.3 | convolution fusion | flops 141603840 | bytes 4902912 | tf_op jit(solution)/shard_map/dot_general | solution.py:17
  106.7 0.0 copy-done.5
  106.8 3.2 %convolution_convert_fusion = bf16[30,1536]{1,0:T(8,128)(2,1)S(1)} fusion(bf16[1536,1536]{1,0:T(8,128)(2,1)} %param.6, f32[30,1536]{1,0:T(8,128)S(1)} %mul.37, bf16[30,1536]{1,0:T(8,128)(2,1)S(1)} %convolution_convert_fusion.1), kind=kOutput, calls=%fused_computation.2 | convolution fusion | flops 141742080 | bytes 5087232 | tf_op jit(solution)/shard_map/dot_general | solution.py:17
  110.0 0.9 reshape.67
  111.0 0.9 copy.45
  111.9 1.6 reduce.2
  113.5 0.1 copy.50
  113.6 0.2 reshape.76
  113.8 36.1 %all_to_all.30 = bf16[64,2,432]{2,1,0:T(2,128)(2,1)S(1)} all-to-all(bf16[64,2,432]{2,1,0:T(2,128)(2,1)S(1)} %reshape.76), channel_id=1, replica_groups=mesh['gz'=64,'gy'=16] {'gz'}, dimensions={0} | all-to-all | bytes 221184 | tf_op jit(solution)/shard_map/all_to_all | solution.py:51
  149.9 0.2 reshape.77
  150.1 1.3 reduce
  151.5 1.6 reshape.68
  153.1 1.2 copy.47
  154.3 1.6 reshape.69
  155.9 0.0 copy-start.3
  155.9 0.1 slice.39
  156.1 0.5 copy-done.3
  156.6 17.0 %all_to_all.31 = bf16[16,48,192]{2,1,0:T(8,128)(2,1)S(1)} all-to-all(bf16[16,48,192]{2,1,0:T(8,128)(2,1)S(1)} %broadcast_in_dim.5), channel_id=1, replica_groups=mesh['gz'=64,'gy'=16] {'gy'}, dimensions={0} | all-to-all | bytes 589824 | tf_op jit(solution)/shard_map/all_to_all | solution.py:13
  173.5 0.1 bitcast_convert_fusion
  173.6 1.1 copy.48
  174.7 0.0 copy-start.2
  174.7 0.0 copy-start.4
  174.7 2.5 %fusion = bf16[768,960]{0,1:T(8,128)(2,1)S(1)} fusion(f32[768,192]{0,1:T(8,128)} %copy.48, bf16[768,768]{1,0:T(8,128)(2,1)S(1)} %copy-done, bf16[768,960]{1,0:T(8,128)(2,1)S(1)} %bitcast.33), kind=kOutput, calls=%fused_computation.1 | convolution fusion | flops 1135411200 | bytes 4718592 | tf_op jit(solution)/shard_map/dot_general | solution.py:17
  177.2 0.0 copy-done.2
  177.2 0.0 copy-done.4
  177.2 0.7 fusion.5
  177.9 0.9 copy.49
  (7 shorter events, 0.2 us)
Async XLA Ops:
  0.0 41.6 %copy-start = (bf16[768,768]{1,0:T(8,128)(2,1)S(1)}, bf16[768,768]{1,0:T(8,128)(2,1)}, u32[]{:S(2)}) copy-start(bf16[768,768]{1,0:T(8,128)(2,1)} %param.7) | copy-start | bytes 3538948
  1.2 40.7 %copy-start.1 = (bf16[48,960]{1,0:T(8,128)(2,1)}, bf16[48,960]{1,0:T(8,128)(2,1)S(1)}, u32[]{:S(2)}) copy-start(bf16[48,960]{1,0:T(8,128)(2,1)S(1)} %copy.35) | copy-start | bytes 276484
  2.5 17.7 %copy-start.6 = (bf16[8,48,24]{1,2,0:T(8,128)(2,1)S(1)}, bf16[8,48,24]{1,2,0:T(8,128)(2,1)}, u32[]{:S(2)}) copy-start(bf16[8,48,24]{1,2,0:T(8,128)(2,1)} %param.5) | copy-start | bytes 55300
  2.5 39.0 %all-to-all-start = ((bf16[16,48,960]{2,1,0:T(8,128)(2,1)}), bf16[16,48,960]{2,1,0:T(8,128)(2,1)S(1)}, u32[]{:S(2)}, u32[]{:S(2)}) async-start(bf16[16,48,960]{2,1,0:T(8,128)(2,1)} %broadcast_in_dim.4), calls=%async_computation | async-start | bytes 3145728 | tf_op jit(solution)/shard_map/all_to_all | solution.py:13
  103.4 3.3 %copy-start.5 = (f32[6,1536]{1,0:T(8,128)S(1)}, f32[6,1536]{1,0:T(8,128)}, u32[]{:S(2)}) copy-start(f32[6,1536]{1,0:T(8,128)} %reshape.71) | copy-start | bytes 110596
  155.9 0.6 copy-start.3
  174.7 2.5 %copy-start.2 = (bf16[48,960]{1,0:T(8,128)(2,1)S(1)}, bf16[48,960]{1,0:T(8,128)(2,1)}, u32[]{:S(2)}) copy-start(bf16[48,960]{1,0:T(8,128)(2,1)} %copy-done.1) | copy-start | bytes 276484
  174.7 2.5 %copy-start.4 = (bf16[48,1152]{1,0:T(8,128)(2,1)S(1)}, bf16[48,1152]{1,0:T(8,128)(2,1)}, u32[]{:S(2)}) copy-start(bf16[48,1152]{1,0:T(8,128)(2,1)} %copy-done.3) | copy-start | bytes 331780

commit v2 on v1

--- a/solution.py
+++ b/solution.py
@@ -17,9 +17,27 @@
     return lax.dot_general(left, right, (dims, ((), ())), preferred_element_type=F32).astype(BF16)
 
 
-def on_device(state, visc_base, dz_op, dy_op):
+def gathered(block):
+    gy = lax.axis_size("gy")
+    held = block[None]
+    for bit in (1, 2):
+        other = lax.ppermute(held, "gy", [(i, i ^ bit) for i in range(gy)])
+        held = jnp.concatenate([held, other], axis=0)
+    parts = [held]
+    for step in range(4, gy, 4):
+        parts.append(lax.ppermute(held, "gy", [(i, (i + step) % gy) for i in range(gy)]))
+    return jnp.concatenate(parts, axis=0)
+
+
+def gathered_order():
+    gy = lax.axis_size("gy")
+    me = lax.axis_index("gy")
+    return [lax.rem((me ^ (k & 3)) + gy - (k & ~3), gy) for k in range(gy)]
+
+
+def section(state, visc_base, dz_op, dy_op):
     fields, planes, ylocal, zlocal = state.shape
-    gz, gy = lax.axis_size("gz"), lax.axis_size("gy")
+    gz = lax.axis_size("gz")
     ny, nz = dy_op.shape[0], dz_op.shape[0]
     parts = gz // planes
     lines = ylocal // parts
@@ -27,16 +45,21 @@
 
     st = jnp.transpose(state, (2, 0, 1, 3)).reshape(ylocal, fields * cols)
     vb = jnp.transpose(visc_base, (1, 0, 2)).reshape(ylocal, cols)
-    whole = spread(st, "gy").reshape(ny, fields * cols)
+    dens = spread(st[:, :cols], "gy").reshape(ny, cols)
     own = lax.dynamic_slice_in_dim(dy_op, lax.axis_index("gy") * ylocal, ylocal, 1)
-    dens_y = rounded(own, whole[:, :cols], ((0,), (0,)))
+    dens_y = rounded(own, dens, ((0,), (0,)))
 
     out = jnp.concatenate([st, dens_y, vb], axis=1)
     out = out.reshape(parts, lines, fields + 2, planes, zlocal)
     out = jnp.transpose(out, (3, 0, 2, 1, 4)).reshape(gz, (fields + 2) * lines * zlocal)
     got = lax.all_to_all(out, "gz", split_axis=0, concat_axis=0, tiled=True)
+    rest = gathered(st[:, cols:]).reshape(ny, (fields - 1) * cols)
+    rows = jnp.concatenate([lax.dynamic_slice_in_dim(dy_op, i * ylocal, ylocal, 0) for i in gathered_order()], axis=0)
+    grad_r = rounded(rows, rest, ((0,), (0,)))
+    grad_d = rounded(dy_op, dens, ((0,), (0,)))
+    grad_y = lax.optimization_barrier(jnp.concatenate([grad_d, grad_r], axis=1))
     got = got.reshape(gz, (fields + 2) * lines, zlocal)
-    got = jnp.transpose(got, (1, 0, 2)).reshape((fields + 2) * lines, nz)
+    got = lax.optimization_barrier(jnp.transpose(got, (1, 0, 2)).reshape((fields + 2) * lines, nz))
     grad_z = rounded(got[: fields * lines], dz_op, ((1,), (0,)))
     gz0 = grad_z[:lines].astype(F32)
     gy0 = got[fields * lines : (fields + 1) * lines].astype(F32)
@@ -52,7 +75,6 @@
     ret = ret.reshape(planes, parts, fields + 1, lines, zlocal)
     ret = jnp.transpose(ret, (1, 3, 2, 0, 4)).reshape(ylocal, (fields + 1) * cols)
 
-    grad_y = rounded(dy_op, whole, ((0,), (0,)))
     visc_all = spread(ret[:, fields * cols :], "gy").reshape(ny, cols)
     flux_y = (visc_all.astype(F32)[:, None] * grad_y.reshape(ny, fields, cols).astype(F32)).astype(BF16)
     div_y = rounded(own, flux_y.reshape(ny, fields * cols), ((0,), (0,)))
@@ -63,7 +85,7 @@
 
 def solution(mesh):
     return jax.shard_map(
-        on_device,
+        section,
         mesh=mesh,
         in_specs=(P(None, None, "gy", "gz"), P(None, "gy", "gz"), P(), P()),
         out_specs=P(None, None, "gy", "gz"),

time: 179 us -> 160 us (0.89)
  blocking collectives: 103 us -> 0 us
  starting transfers between devices: 17.7 us -> 67.2 us
  waiting for transfers between devices: 21.2 us -> 43.9 us
  local copies, waits for them, and re-layouts: 21.8 us -> 31.4 us
    all_to_all x3 -> x0, blocking collectives: 103 us -> none  [the longest x1 49.7 us: on_device(): got = lax.all_to_all(out, 'gz', split_axis=0, concat_axis=0, tiled=True)]
    all_to_all x0 -> x2, waiting for transfers between devices: none -> 28.9 us  [the longest x1 20.9 us: section(): got = lax.all_to_all(out, 'gz', split_axis=0, concat_axis=0, tiled=True)]
    all_to_all x0 -> x2, starting transfers between devices: none -> 27.5 us  [the longest x1 20.8 us: section(): got = lax.all_to_all(out, 'gz', split_axis=0, concat_axis=0, tiled=True)]
    ppermute x0 -> x5, starting transfers between devices: none -> 27.5 us  [the longest x2 18.1 us: gathered(): other = lax.ppermute(held, 'gy', [(i, i ^ bit) for i in range(gy)])]
    unnamed x19 -> x39, local copies, waits for them, and re-layouts: 1.41 us -> 15.4 us
    all_to_all x1 -> x2, waiting for transfers between devices: 21.2 us -> 7.68 us  [spread(): return lax.all_to_all(copies, axis, split_axis=0, concat_axis=0, tiled=True)]
    ppermute x0 -> x5, waiting for transfers between devices: none -> 7.32 us  [the longest x3 7.32 us: gathered(): lax.ppermute(held, 'gy', [(i, (i + step) % gy) for i in range(gy)])]
    all_to_all x1 -> x2, starting transfers between devices: 17.7 us -> 12.3 us  [spread(): return lax.all_to_all(copies, axis, split_axis=0, concat_axis=0, tiled=True)]
  transfers between devices with their start and end apart: 1 -> 9, of which waited for: 1 -> 6; matrix products, arithmetic and copies ran while one was open for 0% -> 23% of each run, Pallas kernels for 0% -> 0%
where the time goes in v2:
time: 160 us
  starting transfers between devices  67.2 us (42%)
  waiting for transfers between devices  43.9 us (27%)
  local copies, waits for them, and re-layouts  31.4 us (20%)
  matrix products  10.3 us (6%)
  other arithmetic  6.3 us (4%)
    all_to_all x1, waiting for transfers between devices, section(): got = lax.all_to_all(out, 'gz', split_axis=0, concat_axis=0, tiled=True)  20.9 us
    all_to_all x1, starting transfers between devices, section(): got = lax.all_to_all(out, 'gz', split_axis=0, concat_axis=0, tiled=True)  20.8 us
    ppermute x2, starting transfers between devices, gathered(): other = lax.ppermute(held, 'gy', [(i, i ^ bit) for i in range(gy)])  18.1 us
    unnamed x39, local copies, waits for them, and re-layouts  15.4 us
    all_to_all x2, starting transfers between devices, spread(): return lax.all_to_all(copies, axis, split_axis=0, concat_axis=0, tiled=True)  12.3 us
    dot_general x6, matrix products, rounded(): lax.dot_general(left, right, (dims, ((), ())), preferred_element_type=F32)  10.3 us
    ppermute x3, starting transfers between devices, gathered(): lax.ppermute(held, 'gy', [(i, (i + step) % gy) for i in range(gy)])  9.35 us
    all_to_all x1, waiting for transfers between devices, section(): ret = lax.all_to_all(ret, 'gz', split_axis=0, concat_axis=0, tiled=True)  7.99 us
  transfers between devices with their start and end apart: 9, of which 6 were waited for; matrix products, arithmetic and copies ran while one was open for 23% of the time, Pallas kernels for 0%

profile of v2, /device:TPU:1, one launch (start us, length us, event | category | flops | bytes accessed | tf_op | source)
XLA Modules:
  0.0 159.6 jit_solution(1323782826480606369)
XLA Ops:
  0.0 1.7 %slice_bitcast_fusion = bf16[1,48,768]{1,2,0:T(8,128)(2,1)} fusion(bf16[48,960]{0,1:T(8,128)(2,1)} %bitcast.46), kind=kLoop, calls=%fused_computation.17 | loop fusion | bytes 147456 | tf_op jit(solution)/shard_map/broadcast_in_dim | solution.py:22
  1.7 16.0 %collective-permute-start = (bf16[1,48,768]{1,2,0:T(8,128)(2,1)}, bf16[1,48,768]{1,2,0:T(8,128)(2,1)}, u32[]{:S(2)}, u32[]{:S(2)}) collective-permute-start(bf16[1,48,768]{1,2,0:T(8,128)(2,1)} %slice_bitcast_fusion), channel_id=1, source_target_pairs={{0,1},{1,0},{2,3},{3,2},{4,5},{5,4},{6,7},{7,6},{8,9},{9,8},{10,11... | collective-permute-start | bytes 221192 | tf_op jit(solution)/shard_map/ppermute | solution.py:24
  17.7 0.8 slice.32
  18.6 0.8 broadcast_in_dim.6
  19.4 3.6 %all-to-all-start = ((bf16[16,48,192]{2,1,0:T(8,128)(2,1)}), bf16[16,48,192]{2,1,0:T(8,128)(2,1)S(1)}, u32[]{:S(2)}, u32[]{:S(2)}) async-start(bf16[16,48,192]{2,1,0:T(8,128)(2,1)} %broadcast_in_dim.6), calls=%async_computation | async-start | bytes 786432 | tf_op jit(solution)/shard_map/all_to_all | solution.py:13
  23.1 1.0 copy.54
  24.1 0.6 constant_dynamic-update-slice_fusion.5
  24.8 0.6 dynamic-slice_dynamic-update-slice_fusion.15
  25.4 0.6 dynamic-slice_dynamic-update-slice_fusion.14
  26.0 0.6 dynamic-slice_dynamic-update-slice_fusion.13
  26.7 0.6 dynamic-slice_dynamic-update-slice_fusion.12
  27.3 0.6 dynamic-slice_dynamic-update-slice_fusion.11
  27.9 0.6 dynamic-slice_dynamic-update-slice_fusion.10
  28.8 0.6 dynamic-slice_dynamic-update-slice_fusion.9
  29.5 0.6 dynamic-slice_dynamic-update-slice_fusion.8
  30.1 1.4 all-to-all-done
  32.0 0.6 reshape.63
  32.8 0.9 all_to_all.24
  33.7 0.6 broadcast.22
  34.3 1.5 reduce.1
  35.7 0.8 reshape.73
  36.5 20.8 %all-to-all-start.1 = ((bf16[64,2,504]{2,1,0:T(2,128)(2,1)}), bf16[64,2,504]{2,1,0:T(2,128)(2,1)S(1)}, u32[]{:S(2)}, u32[]{:S(2)}) async-start(bf16[64,2,504]{2,1,0:T(2,128)(2,1)} %reshape.73), calls=%async_computation.1 | async-start | bytes 262144 | tf_op jit(solution)/shard_map/all_to_all | solution.py:55
  57.3 0.6 dynamic-slice_dynamic-update-slice_fusion.7
  58.0 0.6 dynamic-slice_dynamic-update-slice_fusion.6
  58.6 0.6 dynamic-slice_dynamic-update-slice_fusion.5
  59.3 0.6 dynamic-slice_dynamic-update-slice_fusion.4
  59.9 0.6 dynamic-slice_dynamic-update-slice_fusion.3
  60.5 0.6 dynamic-slice_dynamic-update-slice_fusion.2
  61.1 0.6 dynamic-slice_dynamic-update-slice_fusion.1
  61.8 0.6 dynamic-slice_dynamic-update-slice_fusion
  62.4 1.0 copy.55
  63.5 0.7 pad_maximum_fusion.2
  64.1 2.1 %collective-permute-start.1 = (bf16[2,48,768]{2,1,0:T(8,128)(2,1)}, bf16[2,48,768]{2,1,0:T(8,128)(2,1)S(1)}, u32[]{:S(2)}, u32[]{:S(2)}) collective-permute-start(bf16[2,48,768]{2,1,0:T(8,128)(2,1)} %pad_maximum_fusion.2), channel_id=1, source_target_pairs={{0,2},{1,3},{2,0},{3,1},{4,6},{5,7},{6,4},{7,5},{8,10},{9,11},{10,... | collective-permute-start | bytes 442376 | tf_op jit(solution)/shard_map/ppermute | solution.py:24
  66.2 20.9 %all-to-all-done.1 = bf16[64,2,504]{2,1,0:T(2,128)(2,1)S(1)} async-done(((bf16[64,2,504]{2,1,0:T(2,128)(2,1)}), bf16[64,2,504]{2,1,0:T(2,128)(2,1)S(1)}, u32[]{:S(2)}, u32[]{:S(2)}) %all-to-all-start.1) | async-done | bytes 129056 | tf_op jit(solution)/shard_map/all_to_all | solution.py:55
  88.6 3.3 %convolution_convert_fusion.1 = bf16[30,1536]{1,0:T(8,128)(2,1)S(1)} fusion(bf16[1536,1536]{1,0:T(8,128)(2,1)} %param.6, bf16[42,1536]{0,1:T(8,128)(2,1)S(1)} %bitcast.39), kind=kOutput, calls=%fused_computation.3 | convolution fusion | flops 141603840 | bytes 4939776 | tf_op jit(solution)/shard_map/dot_general | solution.py:17
  92.0 3.2 %convolution_convert_fusion = bf16[30,1536]{1,0:T(8,128)(2,1)S(1)} fusion(bf16[1536,1536]{1,0:T(8,128)(2,1)} %param.6, f32[30,1536]{1,0:T(8,128)S(1)} %mul.85, bf16[30,1536]{1,0:T(8,128)(2,1)S(1)} %convolution_convert_fusion.1), kind=kOutput, calls=%fused_computation.2 | convolution fusion | flops 141742080 | bytes 5087232 | tf_op jit(solution)/shard_map/dot_general | solution.py:17
  95.2 0.9 reshape.66
  96.4 0.8 reduce.2
  97.3 0.8 reshape.75
  98.1 6.7 %all-to-all-start.2 = ((bf16[64,2,432]{2,1,0:T(2,128)(2,1)}), bf16[64,2,432]{2,1,0:T(2,128)(2,1)S(1)}, u32[]{:S(2)}, u32[]{:S(2)}) async-start(bf16[64,2,432]{2,1,0:T(2,128)(2,1)} %reshape.75), calls=%async_computation.2 | async-start | bytes 262144 | tf_op jit(solution)/shard_map/all_to_all | solution.py:74
  104.8 0.6 constant_dynamic-update-slice_fusion.4
  105.5 1.9 %collective-permute-start.2 = (bf16[4,48,768]{2,1,0:T(8,128)(2,1)S(1)}, bf16[4,48,768]{2,1,0:T(8,128)(2,1)S(1)}, u32[]{:S(2)}, u32[]{:S(2)}) collective-permute-start(bf16[4,48,768]{2,1,0:T(8,128)(2,1)S(1)} %pad_maximum_fusion.1), channel_id=1, source_target_pairs={{0,4},{1,5},{2,6},{3,7},{4,8},{5,9},{6,10},{7,11},{8,12},{9,13},{1... | collective-permute-start | bytes 884744 | tf_op jit(solution)/shard_map/ppermute | solution.py:28
  107.4 4.2 %collective-permute-start.3 = (bf16[4,48,768]{2,1,0:T(8,128)(2,1)S(1)}, bf16[4,48,768]{2,1,0:T(8,128)(2,1)S(1)}, u32[]{:S(2)}, u32[]{:S(2)}) collective-permute-start(bf16[4,48,768]{2,1,0:T(8,128)(2,1)S(1)} %pad_maximum_fusion.1), channel_id=1, source_target_pairs={{0,8},{1,9},{2,10},{3,11},{4,12},{5,13},{6,14},{7,15},{8,0},{9,1},... | collective-permute-start | bytes 884744 | tf_op jit(solution)/shard_map/ppermute | solution.py:28
  111.6 3.3 %collective-permute-start.4 = (bf16[4,48,768]{2,1,0:T(8,128)(2,1)S(1)}, bf16[4,48,768]{2,1,0:T(8,128)(2,1)S(1)}, u32[]{:S(2)}, u32[]{:S(2)}) collective-permute-start(bf16[4,48,768]{2,1,0:T(8,128)(2,1)S(1)} %pad_maximum_fusion.1), channel_id=1, source_target_pairs={{0,12},{1,13},{2,14},{3,15},{4,0},{5,1},{6,2},{7,3},{8,4},{9,5},{1... | collective-permute-start | bytes 884744 | tf_op jit(solution)/shard_map/ppermute | solution.py:28
  114.9 0.7 constant_dynamic-update-slice_fusion.3
  115.5 0.4 convolution_convert_fusion.3
  116.0 0.7 constant_dynamic-update-slice_fusion.2
  116.7 4.7 %collective-permute-done.3 = bf16[4,48,768]{2,1,0:T(8,128)(2,1)S(1)} collective-permute-done((bf16[4,48,768]{2,1,0:T(8,128)(2,1)S(1)}, bf16[4,48,768]{2,1,0:T(8,128)(2,1)S(1)}, u32[]{:S(2)}, u32[]{:S(2)}) %collective-permute-start.3) | collective-permute-done | bytes 294944 | tf_op jit(solution)/shard_map/ppermute | solution.py:28
  121.4 0.7 constant_dynamic-update-slice_fusion.1
  122.1 2.6 %collective-permute-done.4 = bf16[4,48,768]{2,1,0:T(8,128)(2,1)S(1)} collective-permute-done((bf16[4,48,768]{2,1,0:T(8,128)(2,1)S(1)}, bf16[4,48,768]{2,1,0:T(8,128)(2,1)S(1)}, u32[]{:S(2)}, u32[]{:S(2)}) %collective-permute-start.4) | collective-permute-done | bytes 294944 | tf_op jit(solution)/shard_map/ppermute | solution.py:28
  124.8 0.7 constant_dynamic-update-slice_fusion
  125.5 8.0 %all-to-all-done.2 = bf16[64,2,432]{2,1,0:T(2,128)(2,1)S(1)} async-done(((bf16[64,2,432]{2,1,0:T(2,128)(2,1)}), bf16[64,2,432]{2,1,0:T(2,128)(2,1)S(1)}, u32[]{:S(2)}, u32[]{:S(2)}) %all-to-all-start.2) | async-done | bytes 110624 | tf_op jit(solution)/shard_map/all_to_all | solution.py:74
  133.7 0.7 reduce
  134.4 0.8 reshape.67
  135.6 0.6 reshape.68
  136.3 0.8 broadcast_in_dim.7
  137.1 8.7 %all-to-all-start.3 = ((bf16[16,48,192]{2,1,0:T(8,128)(2,1)}), bf16[16,48,192]{2,1,0:T(8,128)(2,1)}, u32[]{:S(2)}, u32[]{:S(2)}) async-start(bf16[16,48,192]{2,1,0:T(8,128)(2,1)} %broadcast_in_dim.7), calls=%async_computation.3 | async-start | bytes 786432 | tf_op jit(solution)/shard_map/all_to_all | solution.py:13
  145.7 2.4 %convolution_convert_fusion.2 = bf16[768,768]{0,1:T(8,128)(2,1)S(1)} fusion(bf16[768,768]{1,0:T(8,128)(2,1)S(1)} %copy-done.5, bf16[768,768]{1,0:T(8,128)(2,1)} %bitcast.16), kind=kOutput, calls=%fused_computation.4 | convolution fusion | flops 906559488 | bytes 3538944 | tf_op jit(solution)/shard_map/dot_general | solution.py:17
  148.3 6.2 %all-to-all-done.3 = bf16[16,48,192]{2,1,0:T(8,128)(2,1)} async-done(((bf16[16,48,192]{2,1,0:T(8,128)(2,1)}), bf16[16,48,192]{2,1,0:T(8,128)(2,1)}, u32[]{:S(2)}, u32[]{:S(2)}) %all-to-all-start.3) | async-done | bytes 294944 | tf_op jit(solution)/shard_map/all_to_all | solution.py:13
  154.5 1.0 bitcast_convert_fusion
  155.6 1.1 copy.49
  156.6 1.4 fusion
  158.0 0.7 fusion.5
  158.7 0.9 copy.56
  (38 shorter events, 3.6 us)
Async XLA Ops:
  0.0 24.8 %copy-start = (bf16[768,768]{1,0:T(8,128)(2,1)S(1)}, bf16[768,768]{1,0:T(8,128)(2,1)}, u32[]{:S(2)}) copy-start(bf16[768,768]{1,0:T(8,128)(2,1)} %param.7) | copy-start | bytes 3538948
  1.7 60.7 %collective-permute-start = (bf16[1,48,768]{1,2,0:T(8,128)(2,1)}, bf16[1,48,768]{1,2,0:T(8,128)(2,1)}, u32[]{:S(2)}, u32[]{:S(2)}) collective-permute-start(bf16[1,48,768]{1,2,0:T(8,128)(2,1)} %slice_bitcast_fusion), channel_id=1, source_target_pairs={{0,1},{1,0},{2,3},{3,2},{4,5},{5,4},{6,7},{7,6},{8,9},{9,8},{10,11... | collective-permute-start | bytes 221192 | tf_op jit(solution)/shard_map/ppermute | solution.py:24
  19.4 9.1 %copy-start.1 = (bf16[5,8,48,24]{2,3,1,0:T(8,128)(2,1)S(1)}, bf16[5,8,48,24]{2,3,1,0:T(8,128)(2,1)}, u32[]{:S(2)}) copy-start(bf16[5,8,48,24]{2,3,1,0:T(8,128)(2,1)} %param.4) | copy-start | bytes 276484
  19.4 12.1 %all-to-all-start = ((bf16[16,48,192]{2,1,0:T(8,128)(2,1)}), bf16[16,48,192]{2,1,0:T(8,128)(2,1)S(1)}, u32[]{:S(2)}, u32[]{:S(2)}) async-start(bf16[16,48,192]{2,1,0:T(8,128)(2,1)} %broadcast_in_dim.6), calls=%async_computation | async-start | bytes 786432 | tf_op jit(solution)/shard_map/all_to_all | solution.py:13
  23.0 5.7 %copy-start.4 = (bf16[8,48,24]{1,2,0:T(8,128)(2,1)S(1)}, bf16[8,48,24]{1,2,0:T(8,128)(2,1)}, u32[]{:S(2)}) copy-start(bf16[8,48,24]{1,2,0:T(8,128)(2,1)} %param.5) | copy-start | bytes 55300
  36.5 50.6 %all-to-all-start.1 = ((bf16[64,2,504]{2,1,0:T(2,128)(2,1)}), bf16[64,2,504]{2,1,0:T(2,128)(2,1)S(1)}, u32[]{:S(2)}, u32[]{:S(2)}) async-start(bf16[64,2,504]{2,1,0:T(2,128)(2,1)} %reshape.73), calls=%async_computation.1 | async-start | bytes 262144 | tf_op jit(solution)/shard_map/all_to_all | solution.py:55
  64.1 41.3 %collective-permute-start.1 = (bf16[2,48,768]{2,1,0:T(8,128)(2,1)}, bf16[2,48,768]{2,1,0:T(8,128)(2,1)S(1)}, u32[]{:S(2)}, u32[]{:S(2)}) collective-permute-start(bf16[2,48,768]{2,1,0:T(8,128)(2,1)} %pad_maximum_fusion.2), channel_id=1, source_target_pairs={{0,2},{1,3},{2,0},{3,1},{4,6},{5,7},{6,4},{7,5},{8,10},{9,11},{10,... | collective-permute-start | bytes 442376 | tf_op jit(solution)/shard_map/ppermute | solution.py:24
  98.1 35.4 %all-to-all-start.2 = ((bf16[64,2,432]{2,1,0:T(2,128)(2,1)}), bf16[64,2,432]{2,1,0:T(2,128)(2,1)S(1)}, u32[]{:S(2)}, u32[]{:S(2)}) async-start(bf16[64,2,432]{2,1,0:T(2,128)(2,1)} %reshape.75), calls=%async_computation.2 | async-start | bytes 262144 | tf_op jit(solution)/shard_map/all_to_all | solution.py:74
  105.5 10.5 %collective-permute-start.2 = (bf16[4,48,768]{2,1,0:T(8,128)(2,1)S(1)}, bf16[4,48,768]{2,1,0:T(8,128)(2,1)S(1)}, u32[]{:S(2)}, u32[]{:S(2)}) collective-permute-start(bf16[4,48,768]{2,1,0:T(8,128)(2,1)S(1)} %pad_maximum_fusion.1), channel_id=1, source_target_pairs={{0,4},{1,5},{2,6},{3,7},{4,8},{5,9},{6,10},{7,11},{8,12},{9,13},{1... | collective-permute-start | bytes 884744 | tf_op jit(solution)/shard_map/ppermute | solution.py:28
  107.4 14.0 %collective-permute-start.3 = (bf16[4,48,768]{2,1,0:T(8,128)(2,1)S(1)}, bf16[4,48,768]{2,1,0:T(8,128)(2,1)S(1)}, u32[]{:S(2)}, u32[]{:S(2)}) collective-permute-start(bf16[4,48,768]{2,1,0:T(8,128)(2,1)S(1)} %pad_maximum_fusion.1), channel_id=1, source_target_pairs={{0,8},{1,9},{2,10},{3,11},{4,12},{5,13},{6,14},{7,15},{8,0},{9,1},... | collective-permute-start | bytes 884744 | tf_op jit(solution)/shard_map/ppermute | solution.py:28
  111.6 13.2 %collective-permute-start.4 = (bf16[4,48,768]{2,1,0:T(8,128)(2,1)S(1)}, bf16[4,48,768]{2,1,0:T(8,128)(2,1)S(1)}, u32[]{:S(2)}, u32[]{:S(2)}) collective-permute-start(bf16[4,48,768]{2,1,0:T(8,128)(2,1)S(1)} %pad_maximum_fusion.1), channel_id=1, source_target_pairs={{0,12},{1,13},{2,14},{3,15},{4,0},{5,1},{6,2},{7,3},{8,4},{9,5},{1... | collective-permute-start | bytes 884744 | tf_op jit(solution)/shard_map/ppermute | solution.py:28
  136.2 12.0 %copy-start.2 = (bf16[48,1152]{1,0:T(8,128)(2,1)}, bf16[48,1152]{1,0:T(8,128)(2,1)S(1)}, u32[]{:S(2)}) copy-start(bf16[48,1152]{1,0:T(8,128)(2,1)S(1)} %reshape.68) | copy-start | bytes 331780
  136.2 9.6 %copy-start.5 = (bf16[768,768]{1,0:T(8,128)(2,1)S(1)}, bf16[768,768]{1,0:T(8,128)(2,1)}, u32[]{:S(2)}) copy-start(bf16[768,768]{1,0:T(8,128)(2,1)} %dynamic-slice_dynamic-update-slice_fusion) | copy-start | bytes 3538948
  137.1 17.4 %all-to-all-start.3 = ((bf16[16,48,192]{2,1,0:T(8,128)(2,1)}), bf16[16,48,192]{2,1,0:T(8,128)(2,1)}, u32[]{:S(2)}, u32[]{:S(2)}) async-start(bf16[16,48,192]{2,1,0:T(8,128)(2,1)} %broadcast_in_dim.7), calls=%async_computation.3 | async-start | bytes 786432 | tf_op jit(solution)/shard_map/all_to_all | solution.py:13
  156.6 1.4 copy-start.3
